TPU v7x, 256 devices: a whole 4x4x8 slice. The times are simulated.
256 devices in a mesh: mom: 4 (over x_hi, core), energy: 64 (over y, z, x_lo).
Axes of the slice: x: 4 (x_hi: 2, x_lo: 2; x = x_hi * 2 + x_lo), y: 4, z: 8, core: 2. Of those that a mesh axis runs over, the one named last changes fastest.
Arguments:
- green: float32 [512, 4, 24, 768], P('energy', 'mom'), may hold values from -6 to 6
- gradients: float32 [3, 12, 768], replicated, may hold values from -1.75 to 1.75
- neighbours: int32 [3, 64], replicated, may hold values from 0 to 63
- phonons: float32 [2, 3, 8, 4], replicated, may hold values from 0.02 to 0.2
- offsets: int32 [8], replicated, may hold values from 1 to 8, as said below
Outputs:
- sigma: float32 [512, 4, 24, 768], P('energy', 'mom')
Inputs may be any that keep to these rules, and one draw needn't show every extreme that they name: `offsets`: some frequency takes exactly 8 energy steps.
All inputs are finite; a program needn't handle non-finite values.
Results may differ from a plain program's by a relative error of at most 0.0001.
Values sent between devices are 32-bit elements; how exact they have to be, the bound alone decides.
No kernel may reach another device: no remote copies, remote signals or barrier semaphores. Data moves between devices by JAX's collectives and lax.ppermute only.
A program may use at most 128 MiB of HBM per device.

v0:
```python
import functools

import jax
import jax.numpy as jnp
from jax import lax
from jax.experimental import pallas as pl
from jax.experimental.pallas import tpu as pltpu
from jax.sharding import PartitionSpec as P


ORB = 12
NA = 64
DIRS = 3
NW = 8
HW = 8
NK = 4
WIDTH = ORB * NA
PAIRS = WIDTH // 128
UNROLL_RIGHT = 2
GROUP = 4 * HW

PARAMS = pltpu.CompilerParams(vmem_limit_bytes=24 * 1024 * 1024)


def split_kernel(green_ref, mine_ref, other_ref, staged_ref, sems):
    half = lax.axis_index("mom") // 2

    def fetch(j):
        lanes = pl.ds(j * 128, 128)
        return pltpu.make_async_copy(green_ref.at[:, lanes], staged_ref.at[j], sems.at[j])

    for j in range(PAIRS):
        fetch(j).start()
    for j in range(PAIRS):
        fetch(j).wait()
        lanes = pl.ds(j * 128, 128)
        for part in range(2):

            @pl.when(half == part)
            def _():
                for i in range(ORB):
                    mine_ref[i, :, lanes] = staged_ref[j, pl.ds(part * ORB + i, HW, stride=2 * ORB), :]
                    other_ref[i, :, lanes] = staged_ref[
                        j, pl.ds((1 - part) * ORB + i, HW, stride=2 * ORB), :
                    ]


def prepare_kernel(
    phonons_ref, offsets_ref, neighbours_ref, gradients_ref, lhs_ref, left_ref, right_ref, pick_ref, rows_ref
):
    pick_ref[pl.ds(0, DIRS), pl.ds(0, NA)] = neighbours_ref[...]
    pick_ref[pl.ds(0, DIRS), pl.ds(NA, NA)] = neighbours_ref[...] + NA
    low = lax.broadcasted_iota(jnp.int32, (ORB, 128), 1) < NA
    for d in range(DIRS):
        for jj in range(PAIRS):
            lanes = pl.ds(jj * 128, 128)
            rows = gradients_ref[d, :, lanes]
            swapped = pltpu.roll(rows, NA, 1)
            left_ref[2 * jj, d, pl.ds(0, ORB), :] = jnp.where(low, rows, swapped)
            left_ref[2 * jj + 1, d, pl.ds(0, ORB), :] = jnp.where(low, swapped, rows)
            rows_ref[pl.ds(0, ORB), :] = rows
            even = rows_ref[pl.ds(0, ORB // 2, stride=2), :]
            odd = rows_ref[pl.ds(1, ORB // 2, stride=2), :]
            first = low[: ORB // 2]
            right_ref[d, jj, 0, pl.ds(0, ORB // 2), :] = jnp.where(first, even, odd)
            right_ref[d, jj, 1, pl.ds(0, ORB // 2), :] = jnp.where(
                first, pltpu.roll(even, NA, 1), pltpu.roll(odd, NA, 1)
            )
    mom = lax.axis_index("mom")
    ahead = jnp.where(lax.axis_index("energy") % 2 == 0, HW, -HW)
    shape = (HW, 384)
    row = lax.broadcasted_iota(jnp.int32, shape, 0)
    col = lax.broadcasted_iota(jnp.int32, shape, 1)
    edge = col < 256
    there = edge & (col % 64 >= 32)
    shift = jnp.where(edge, jnp.where(there, -ahead, ahead), 0)
    delta = row - col % 8 + shift
    source = mom ^ ((col // 8) % 4)
    depth = jnp.where(edge, 64, 32)
    fine = col % 256 >= 2 * depth
    for k in range(2):
        circle = ((mom ^ (2 * k)) - source) & 3
        blocks = []
        for d in range(DIRS):
            total = jnp.zeros(shape, jnp.float32)
            for w in range(NW):
                offset = offsets_ref[w]
                for side in range(2):
                    value = jnp.full(shape, phonons_ref[side, d, 0, w], jnp.float32)
                    for n in range(1, NK):
                        value = jnp.where(circle == n, phonons_ref[side, d, n, w], value)
                    hit = delta == (offset if side == 0 else -offset)
                    total = total + jnp.where(hit, value, 0.0)
            top = total.astype(jnp.bfloat16).astype(jnp.float32)
            blocks.append(jnp.where(fine, total - top, top))
        blocks.append(jnp.zeros(shape, jnp.float32))
        lhs_ref[pl.ds(k * GROUP, GROUP), :] = jnp.concatenate(blocks, axis=0).astype(jnp.bfloat16)


def left_products(picked, left_ref, half_ref, d, k, start, lanes):
    for p in range(half_ref.shape[2]):
        total = None
        for i in range(ORB):
            term = left_ref[i, d, pl.ds(start + p, HW, stride=0), :] * picked[i]
            total = term if total is None else total + term
        half_ref[d, k, p, 0, :, lanes] = total
        half_ref[d, k, p, 1, :, lanes] = pltpu.roll(total, NA, 1)


def right_products(right_ref, half_ref, outs):
    for k, out_ref in enumerate(outs):

        def right_side(p, carry):
            sums = [None] * PAIRS
            for d in range(DIRS):
                plain, swapped = (
                    [half_ref[d, k, p, n, :, pl.ds(jj * 128, 128)] for jj in range(PAIRS)] for n in range(2)
                )
                for q in range(PAIRS):
                    for jj in range(PAIRS):
                        straight = right_ref[d, jj, 0, pl.ds(q, HW, stride=0), :]
                        crossed = right_ref[d, jj, 1, pl.ds(q, HW, stride=0), :]
                        term = straight * plain[jj] + crossed * swapped[jj]
                        sums[q] = term if sums[q] is None else sums[q] + term
            for q in range(PAIRS):
                out_ref[p, :, pl.ds(q * 128, 128)] = sums[q]
            return carry

        lax.fori_loop(0, out_ref.shape[0], right_side, 0, unroll=UNROLL_RIGHT)


def mix_kernel(count, first, moms, keep, *refs):
    sources = refs[:count]
    lhs_ref, left_ref, right_ref, pick_ref, *outs = refs[count:-2]
    mixed_ref, half_ref = refs[-2:]
    kept_ref = outs.pop() if keep else None
    depth = count * HW
    rows = len(moms) * GROUP

    def mix(jj, slot):
        lanes = pl.ds(pl.multiple_of(jj * 128, 128), 128)
        weights = lhs_ref[pl.ds(moms[0] * GROUP, rows), first : first + 3 * depth]
        for i in range(0, ORB, 2):
            block = jnp.concatenate(
                [
                    jnp.concatenate([source[i + n, :, lanes] for source in sources], axis=0)
                    for n in range(2)
                ],
                axis=1,
            )
            top = block.astype(jnp.bfloat16)
            rest = (block - top.astype(jnp.float32)).astype(jnp.bfloat16)
            product = jnp.dot(
                weights,
                jnp.concatenate([top, rest, top], axis=0),
                preferred_element_type=jnp.float32,
            )
            for k in range(len(moms)):
                for d in range(DIRS):
                    at = k * GROUP + d * HW
                    total = product[at : at + HW]
                    mixed_ref[slot, i, k, d] = total[:, :128]
                    mixed_ref[slot, i + 1, k, d] = total[:, 128:]

    def left_side(jj, slot):
        lanes = pl.ds(pl.multiple_of(jj * 128, 128), 128)
        for d in range(DIRS):
            pick = pick_ref[pl.ds(d, HW, stride=0), :]
            for k in range(len(moms)):
                picked = [
                    jnp.take_along_axis(
                        mixed_ref[slot, i, k, d], pick, axis=1, mode="promise_in_bounds"
                    )
                    for i in range(ORB)
                ]
                if keep:
                    for i in range(ORB):
                        kept_ref[jj, d, k, i] = picked[i]
                left_products(picked, left_ref, half_ref, d, k, 0, lanes)

    mix(0, 0)

    def step(t, carry):
        mix(2 * t + 1, 1)
        left_side(2 * t, 0)
        mix(jnp.minimum(2 * t + 2, PAIRS - 1), 0)
        left_side(2 * t + 1, 1)
        return carry

    lax.fori_loop(0, PAIRS // 2, step, 0)
    right_products(right_ref, half_ref, outs)


def join_kernel(own_ref, far_ref, near_edge_ref, far_edge_ref, out_ref, staged_ref, sems):
    half = lax.axis_index("mom") // 2

    def flush(j):
        lanes = pl.ds(j * 128, 128)
        return pltpu.make_async_copy(staged_ref.at[j], out_ref.at[:, lanes], sems.at[j])

    for j in range(PAIRS):
        lanes = pl.ds(j * 128, 128)
        for part in range(2):

            @pl.when(half == part)
            def _():
                for p in range(ORB):
                    staged_ref[j, pl.ds(part * ORB + p, HW, stride=2 * ORB), :] = (
                        own_ref[p, :, lanes] + near_edge_ref[p, :, lanes]
                    )
                    staged_ref[j, pl.ds((1 - part) * ORB + p, HW, stride=2 * ORB), :] = (
                        far_ref[p, :, lanes] + far_edge_ref[p, :, lanes]
                    )

        flush(j).start()
    for j in range(PAIRS):
        flush(j).wait()


def send(x, energy_of, flip):
    energies = lax.axis_size("energy")
    moms = lax.axis_size("mom")
    pairs = []
    for m in range(moms):
        for e in range(energies):
            to = energy_of(e)
            if 0 <= to < energies:
                pairs.append((m * energies + e, (m ^ flip) * energies + to))
    return lax.ppermute(x, ("mom", "energy"), pairs)


def stay(e):
    return e


def beyond(e):
    return e - 2 if e % 2 == 0 else e + 2


def pair(e):
    return e ^ 1


VMEM = pl.BlockSpec(memory_space=pltpu.VMEM)
SMEM = pl.BlockSpec(memory_space=pltpu.SMEM)
HBM = pl.BlockSpec(memory_space=pltpu.MemorySpace.HBM)
STAGED = [pltpu.VMEM((PAIRS, HW * 2 * ORB, 128), jnp.float32), pltpu.SemaphoreType.DMA((PAIRS,))]
BLOCK = jax.ShapeDtypeStruct((ORB, HW, WIDTH), jnp.float32)


def mix_call(sources, tables, first, moms, orbitals, keep=False):
    count = len(sources)
    outs = [jax.ShapeDtypeStruct((orbitals, HW, WIDTH), jnp.float32)] * len(moms)
    if keep:
        outs.append(jax.ShapeDtypeStruct((PAIRS, DIRS, len(moms), ORB, HW, 128), jnp.float32))
    return pl.pallas_call(
        functools.partial(mix_kernel, count, first, moms, keep),
        out_shape=tuple(outs),
        in_specs=[VMEM] * (count + 4),
        out_specs=(VMEM,) * len(outs),
        scratch_shapes=[
            pltpu.VMEM((2, ORB, len(moms), DIRS, HW, 128), jnp.float32),
            pltpu.VMEM((DIRS, len(moms), orbitals, 2, HW, WIDTH), jnp.float32),
        ],
        compiler_params=PARAMS,
        name="mix",
    )(*sources, *tables)


def layer(green, gradients, neighbours, phonons, offsets):
    mine, other = pl.pallas_call(
        split_kernel,
        out_shape=(BLOCK, BLOCK),
        in_specs=[HBM],
        out_specs=(VMEM, VMEM),
        scratch_shapes=STAGED,
        compiler_params=PARAMS,
        name="split",
    )(green.reshape(HW * 2 * ORB, WIDTH))
    here_far = send(other, stay, 2)
    beyond_own = send(mine, beyond, 0)
    here_near = send(mine, stay, 1)
    tables = pl.pallas_call(
        prepare_kernel,
        out_shape=(
            jax.ShapeDtypeStruct((2 * GROUP, 384), jnp.bfloat16),
            jax.ShapeDtypeStruct((ORB, DIRS, 16, 128), jnp.float32),
            jax.ShapeDtypeStruct((DIRS, PAIRS, 2, 8, 128), jnp.float32),
            jax.ShapeDtypeStruct((8, 128), jnp.int32),
        ),
        in_specs=[SMEM, SMEM, VMEM, VMEM],
        out_specs=(VMEM,) * 4,
        scratch_shapes=[pltpu.VMEM((16, 128), jnp.float32)],
        compiler_params=PARAMS,
        name="prepare",
    )(phonons.transpose(0, 1, 3, 2), offsets, neighbours, gradients)
    here_far, *tables = lax.optimization_barrier((here_far, *tables))
    beyond_far = send(here_far, beyond, 0)
    here_last = send(here_far, stay, 1)
    here = [mine, here_near, here_far, here_last]
    (far,) = mix_call(here, tables, 256, (1,), ORB)
    _, beyond_own, beyond_far = lax.optimization_barrier((far, beyond_own, beyond_far))
    far = send(far, stay, 2)
    there = [beyond_own, send(beyond_own, stay, 1), beyond_far, send(beyond_far, stay, 1)]
    near_edge, far_edge = mix_call(here + there, tables, 0, (0, 1), ORB)
    edges = [send(near_edge, pair, 0), send(far_edge, pair, 2)]
    here[0], near_edge = lax.optimization_barrier((mine, near_edge))
    (own,) = mix_call(here, tables, 256, (0,), ORB)
    out = pl.pallas_call(
        join_kernel,
        out_shape=jax.ShapeDtypeStruct((HW * 2 * ORB, WIDTH), jnp.float32),
        in_specs=[VMEM] * 4,
        out_specs=HBM,
        scratch_shapes=STAGED,
        compiler_params=PARAMS,
        name="join",
    )(own, far, *edges)
    return out.reshape(green.shape)


def solution(mesh):
    placed = (P("energy", "mom", None, None), P(), P(), P(), P())
    return jax.shard_map(
        layer,
        mesh=mesh,
        in_specs=placed,
        out_specs=P("energy", "mom", None, None),
        check_vma=False,
    )
```

profile of v0, /device:TPU:24, one launch (start us, length us, event | category | flops | bytes accessed | tf_op | source)
XLA Modules:
  0.0 52.8 jit_solution(14133198741157752271)
XLA Ops:
  0.0 0.0 copy-start
  0.0 1.1 %copy-done = f32[8,1,24,768]{3,2,1,0:T(8,128)S(1)} copy-done((f32[8,1,24,768]{3,2,1,0:T(8,128)S(1)}, f32[8,1,24,768]{3,2,1,0:T(8,128)}, u32[]{:S(2)}) %copy-start) | copy-done | bytes 589848
  1.1 0.0 copy-start.1
  1.1 0.0 copy-start.2
  1.1 0.2 split.1
  1.3 0.0 copy-start.3
  1.3 3.1 %collective-permute-start.1 = (f32[12,8,768]{2,1,0:T(8,128)S(1)}, f32[12,8,768]{2,1,0:T(8,128)S(1)}, u32[]{:S(2)}, u32[]{:S(2)}) collective-permute-start(f32[12,8,768]{2,1,0:T(8,128)S(1)} %get-tuple-element.22), channel_id=1, source_target_pairs={{0,128},{1,129},{2,130},{3,131},{4,132},{5,133},{6,134},{7,135},{8... | collective-permute-start | bytes 884744 | tf_op jit(solution)/shard_map/ppermute | solution.py:229
  4.4 0.0 copy-start.4
  4.4 0.0 collective-permute-start
  4.4 0.0 copy-done.1
  4.5 0.0 copy-done.2
  4.5 0.0 copy-done.3
  4.5 0.6 %copy-done.4 = s32[8]{0:T(128)S(1)} copy-done((s32[8]{0:T(128)S(1)}, s32[8]{0:T(128)}, u32[]{:S(2)}) %copy-start.4) | copy-done | bytes 56
  5.1 1.2 %prepare.1 = (bf16[64,384]{1,0:T(8,128)(2,1)S(1)}, f32[12,3,16,128]{3,2,1,0:T(8,128)S(1)}, f32[3,6,2,8,128]{4,3,2,1,0:T(8,128)S(1)}, s32[8,128]{1,0:T(8,128)S(1)}) custom-call(f32[2,3,4,8]{3,2,1,0:T(4,128)S(1)} %bitcast.6, s32[8]{0:T(128)S(1)} %copy-done.4, s32[3,64]{1,0:T(4,128)S(1)} %copy-done.3, f32[3,12,768]{2,1,0:T(8,128)S(1)} %copy-done.1), custom_call_target="tpu_custom_call" | custom-call | tf_op jit(solution)/shard_map/prepare/pallas_call | solution.py:283
  6.3 5.3 %collective-permute-done.1.refs_2_ = f32[12,8,768]{2,1,0:T(8,128)S(1)} collective-permute-done((f32[12,8,768]{2,1,0:T(8,128)S(1)}, f32[12,8,768]{2,1,0:T(8,128)S(1)}, u32[]{:S(2)}, u32[]{:S(2)}) %collective-permute-start.1) | collective-permute-done | bytes 294944 | tf_op jit(solution)/shard_map/ppermute | solution.py:229
  11.7 0.0 collective-permute-start.2
  11.7 7.9 %collective-permute-start.3 = (f32[12,8,768]{2,1,0:T(8,128)S(1)}, f32[12,8,768]{2,1,0:T(8,128)S(1)}, u32[]{:S(2)}, u32[]{:S(2)}) collective-permute-start(f32[12,8,768]{2,1,0:T(8,128)S(1)} %get-tuple-element.35.refs_0_), channel_id=1, source_target_pairs={{1,3},{2,0},{3,5},{4,2},{5,7},{6,4},{7,9},{8,6},{9,11},{10,8},{11,... | collective-permute-start | bytes 884744 | tf_op jit(solution)/shard_map/ppermute | solution.py:229
  19.6 2.9 %collective-permute-start.4 = (f32[12,8,768]{2,1,0:T(8,128)S(1)}, f32[12,8,768]{2,1,0:T(8,128)S(1)}, u32[]{:S(2)}, u32[]{:S(2)}) collective-permute-start(f32[12,8,768]{2,1,0:T(8,128)S(1)} %collective-permute-done.1.refs_2_), channel_id=1, source_target_pairs={{1,3},{2,0},{3,5},{4,2},{5,7},{6,4},{7,9},{8,6},{9,11},{10,8},{11,... | collective-permute-start | bytes 884744 | tf_op jit(solution)/shard_map/ppermute | solution.py:229
  22.5 0.0 collective-permute-done.refs_1_
  22.6 0.0 collective-permute-done.2.refs_3_
  22.6 2.4 %mix.3 = f32[12,8,768]{2,1,0:T(8,128)S(1)} custom-call(f32[12,8,768]{2,1,0:T(8,128)S(1)} %get-tuple-element.35.refs_0_, f32[12,8,768]{2,1,0:T(8,128)S(1)} %collective-permute-done.refs_1_, f32[12,8,768]{2,1,0:T(8,128)S(1)} %collective-permute-done.1.refs_2_, f32[12,8,768]{2,1,0:T(8,128)S(1)} %collective-permute-done.2.refs_3_, ...), custom_call_target="tpu_custom_call" | custom-call | tf_op jit(solution)/shard_map/mix/pallas_call | solution.py:256
  25.0 2.0 %collective-permute-done.3.refs_4_ = f32[12,8,768]{2,1,0:T(8,128)S(1)} collective-permute-done((f32[12,8,768]{2,1,0:T(8,128)S(1)}, f32[12,8,768]{2,1,0:T(8,128)S(1)}, u32[]{:S(2)}, u32[]{:S(2)}) %collective-permute-start.3) | collective-permute-done | bytes 294944 | tf_op jit(solution)/shard_map/ppermute | solution.py:229
  27.0 5.9 %collective-permute-done.4.refs_6_ = f32[12,8,768]{2,1,0:T(8,128)S(1)} collective-permute-done((f32[12,8,768]{2,1,0:T(8,128)S(1)}, f32[12,8,768]{2,1,0:T(8,128)S(1)}, u32[]{:S(2)}, u32[]{:S(2)}) %collective-permute-start.4) | collective-permute-done | bytes 294944 | tf_op jit(solution)/shard_map/ppermute | solution.py:229
  32.9 0.0 collective-permute-start.5
  32.9 0.5 collective-permute-start.6
  33.4 3.0 %collective-permute-start.7 = (f32[12,8,768]{2,1,0:T(8,128)S(1)}, f32[12,8,768]{2,1,0:T(8,128)S(1)}, u32[]{:S(2)}, u32[]{:S(2)}) collective-permute-start(f32[12,8,768]{2,1,0:T(8,128)S(1)} %mix.3), channel_id=1, source_target_pairs={{0,128},{1,129},{2,130},{3,131},{4,132},{5,133},{6,134},{7,135},{8... | collective-permute-start | bytes 884744 | tf_op jit(solution)/shard_map/ppermute | solution.py:229
  36.4 0.0 collective-permute-done.5.refs_5_
  36.4 0.0 collective-permute-done.6.refs_7_
  36.4 4.7 %mix.4 = (f32[12,8,768]{2,1,0:T(8,128)S(1)}, f32[12,8,768]{2,1,0:T(8,128)S(1)}) custom-call(f32[12,8,768]{2,1,0:T(8,128)S(1)} %get-tuple-element.35.refs_0_, f32[12,8,768]{2,1,0:T(8,128)S(1)} %collective-permute-done.refs_1_, f32[12,8,768]{2,1,0:T(8,128)S(1)} %collective-permute-done.1.refs_2_, f32[12,8,768]{2,1,0:T(8,128)S(1)} %collective-permute-done.2.refs_3_, ...), custom_call_target="tpu_custom_call" | custom-call | tf_op jit(solution)/shard_map/mix/pallas_call | solution.py:256
  41.1 2.0 %collective-permute-start.9 = (f32[12,8,768]{2,1,0:T(8,128)S(1)}, f32[12,8,768]{2,1,0:T(8,128)S(1)}, u32[]{:S(2)}, u32[]{:S(2)}) collective-permute-start(f32[12,8,768]{2,1,0:T(8,128)S(1)} %get-tuple-element.36), channel_id=1, source_target_pairs={{0,129},{1,128},{2,131},{3,130},{4,133},{5,132},{6,135},{7,134},{8... | collective-permute-start | bytes 884744 | tf_op jit(solution)/shard_map/ppermute | solution.py:229
  43.1 0.0 collective-permute-start.8
  43.1 2.4 %mix.5.own_ref = f32[12,8,768]{2,1,0:T(8,128)S(1)} custom-call(f32[12,8,768]{2,1,0:T(8,128)S(1)} %get-tuple-element.35.refs_0_, f32[12,8,768]{2,1,0:T(8,128)S(1)} %collective-permute-done.refs_1_, f32[12,8,768]{2,1,0:T(8,128)S(1)} %collective-permute-done.1.refs_2_, f32[12,8,768]{2,1,0:T(8,128)S(1)} %collective-permute-done.2.refs_3_, ...), custom_call_target="tpu_custom_call" | custom-call | tf_op jit(solution)/shard_map/mix/pallas_call | solution.py:256
  45.5 0.0 collective-permute-done.7.far_ref
  45.6 5.5 %collective-permute-done.9.far_edge_ref = f32[12,8,768]{2,1,0:T(8,128)S(1)} collective-permute-done((f32[12,8,768]{2,1,0:T(8,128)S(1)}, f32[12,8,768]{2,1,0:T(8,128)S(1)}, u32[]{:S(2)}, u32[]{:S(2)}) %collective-permute-start.9) | collective-permute-done | bytes 294944 | tf_op jit(solution)/shard_map/ppermute | solution.py:229
  51.0 0.9 %collective-permute-done.8.near_edge_ref = f32[12,8,768]{2,1,0:T(8,128)S(1)} collective-permute-done((f32[12,8,768]{2,1,0:T(8,128)S(1)}, f32[12,8,768]{2,1,0:T(8,128)S(1)}, u32[]{:S(2)}, u32[]{:S(2)}) %collective-permute-start.8) | collective-permute-done | bytes 294944 | tf_op jit(solution)/shard_map/ppermute | solution.py:229
  51.9 0.9 %join.1 = f32[192,768]{1,0:T(8,128)} custom-call(f32[12,8,768]{2,1,0:T(8,128)S(1)} %mix.5.own_ref, f32[12,8,768]{2,1,0:T(8,128)S(1)} %collective-permute-done.7.far_ref, f32[12,8,768]{2,1,0:T(8,128)S(1)} %collective-permute-done.8.near_edge_ref, f32[12,8,768]{2,1,0:T(8,128)S(1)} %collective-permute-done.9.far_edge_ref), custom_call_target="tpu_custom_call" | custom-call | tf_op jit(solution)/shard_map/join/pallas_call | solution.py:309
Async XLA Ops:
  0.0 1.1 %copy-start = (f32[8,1,24,768]{3,2,1,0:T(8,128)S(1)}, f32[8,1,24,768]{3,2,1,0:T(8,128)}, u32[]{:S(2)}) copy-start(f32[8,1,24,768]{3,2,1,0:T(8,128)} %param.5) | copy-start | bytes 1769476
  1.1 3.4 %copy-start.1 = (f32[3,12,768]{2,1,0:T(8,128)S(1)}, f32[3,12,768]{2,1,0:T(8,128)}, u32[]{:S(2)}) copy-start(f32[3,12,768]{2,1,0:T(8,128)} %gradients_ref.1) | copy-start | bytes 331780
  1.1 3.4 %copy-start.2 = (f32[2,3,8,4]{2,3,1,0:T(4,128)S(1)}, f32[2,3,8,4]{2,3,1,0:T(4,128)}, u32[]{:S(2)}) copy-start(f32[2,3,8,4]{2,3,1,0:T(4,128)} %param.8) | copy-start | bytes 2308
  1.3 3.1 %copy-start.3 = (s32[3,64]{1,0:T(4,128)S(1)}, s32[3,64]{1,0:T(4,128)}, u32[]{:S(2)}) copy-start(s32[3,64]{1,0:T(4,128)} %neighbours_ref.1) | copy-start | bytes 2308
  1.3 10.3 %collective-permute-start.1 = (f32[12,8,768]{2,1,0:T(8,128)S(1)}, f32[12,8,768]{2,1,0:T(8,128)S(1)}, u32[]{:S(2)}, u32[]{:S(2)}) collective-permute-start(f32[12,8,768]{2,1,0:T(8,128)S(1)} %get-tuple-element.22), channel_id=1, source_target_pairs={{0,128},{1,129},{2,130},{3,131},{4,132},{5,133},{6,134},{7,135},{8... | collective-permute-start | bytes 884744 | tf_op jit(solution)/shard_map/ppermute | solution.py:229
  4.4 0.7 %copy-start.4 = (s32[8]{0:T(128)S(1)}, s32[8]{0:T(128)}, u32[]{:S(2)}) copy-start(s32[8]{0:T(128)} %offsets_ref.1) | copy-start | bytes 100
  4.4 18.1 %collective-permute-start = (f32[12,8,768]{2,1,0:T(8,128)S(1)}, f32[12,8,768]{2,1,0:T(8,128)S(1)}, u32[]{:S(2)}, u32[]{:S(2)}) collective-permute-start(f32[12,8,768]{2,1,0:T(8,128)S(1)} %get-tuple-element.35.refs_0_), channel_id=1, source_target_pairs={{0,64},{1,65},{2,66},{3,67},{4,68},{5,69},{6,70},{7,71},{8,72},{9,... | collective-permute-start | bytes 884744 | tf_op jit(solution)/shard_map/ppermute | solution.py:229
  11.7 10.9 %collective-permute-start.2 = (f32[12,8,768]{2,1,0:T(8,128)S(1)}, f32[12,8,768]{2,1,0:T(8,128)S(1)}, u32[]{:S(2)}, u32[]{:S(2)}) collective-permute-start(f32[12,8,768]{2,1,0:T(8,128)S(1)} %collective-permute-done.1.refs_2_), channel_id=1, source_target_pairs={{0,64},{1,65},{2,66},{3,67},{4,68},{5,69},{6,70},{7,71},{8,72},{9,... | collective-permute-start | bytes 884744 | tf_op jit(solution)/shard_map/ppermute | solution.py:229
  11.7 15.3 %collective-permute-start.3 = (f32[12,8,768]{2,1,0:T(8,128)S(1)}, f32[12,8,768]{2,1,0:T(8,128)S(1)}, u32[]{:S(2)}, u32[]{:S(2)}) collective-permute-start(f32[12,8,768]{2,1,0:T(8,128)S(1)} %get-tuple-element.35.refs_0_), channel_id=1, source_target_pairs={{1,3},{2,0},{3,5},{4,2},{5,7},{6,4},{7,9},{8,6},{9,11},{10,8},{11,... | collective-permute-start | bytes 884744 | tf_op jit(solution)/shard_map/ppermute | solution.py:229
  19.6 13.2 %collective-permute-start.4 = (f32[12,8,768]{2,1,0:T(8,128)S(1)}, f32[12,8,768]{2,1,0:T(8,128)S(1)}, u32[]{:S(2)}, u32[]{:S(2)}) collective-permute-start(f32[12,8,768]{2,1,0:T(8,128)S(1)} %collective-permute-done.1.refs_2_), channel_id=1, source_target_pairs={{1,3},{2,0},{3,5},{4,2},{5,7},{6,4},{7,9},{8,6},{9,11},{10,8},{11,... | collective-permute-start | bytes 884744 | tf_op jit(solution)/shard_map/ppermute | solution.py:229
  32.9 3.5 %collective-permute-start.5 = (f32[12,8,768]{2,1,0:T(8,128)S(1)}, f32[12,8,768]{2,1,0:T(8,128)S(1)}, u32[]{:S(2)}, u32[]{:S(2)}) collective-permute-start(f32[12,8,768]{2,1,0:T(8,128)S(1)} %collective-permute-done.3.refs_4_), channel_id=1, source_target_pairs={{0,64},{1,65},{2,66},{3,67},{4,68},{5,69},{6,70},{7,71},{8,72},{9,... | collective-permute-start | bytes 884744 | tf_op jit(solution)/shard_map/ppermute | solution.py:229
  32.9 3.5 %collective-permute-start.6 = (f32[12,8,768]{2,1,0:T(8,128)S(1)}, f32[12,8,768]{2,1,0:T(8,128)S(1)}, u32[]{:S(2)}, u32[]{:S(2)}) collective-permute-start(f32[12,8,768]{2,1,0:T(8,128)S(1)} %collective-permute-done.4.refs_6_), channel_id=1, source_target_pairs={{0,64},{1,65},{2,66},{3,67},{4,68},{5,69},{6,70},{7,71},{8,72},{9,... | collective-permute-start | bytes 884744 | tf_op jit(solution)/shard_map/ppermute | solution.py:229
  33.4 12.2 %collective-permute-start.7 = (f32[12,8,768]{2,1,0:T(8,128)S(1)}, f32[12,8,768]{2,1,0:T(8,128)S(1)}, u32[]{:S(2)}, u32[]{:S(2)}) collective-permute-start(f32[12,8,768]{2,1,0:T(8,128)S(1)} %mix.3), channel_id=1, source_target_pairs={{0,128},{1,129},{2,130},{3,131},{4,132},{5,133},{6,134},{7,135},{8... | collective-permute-start | bytes 884744 | tf_op jit(solution)/shard_map/ppermute | solution.py:229
  41.1 9.9 %collective-permute-start.9 = (f32[12,8,768]{2,1,0:T(8,128)S(1)}, f32[12,8,768]{2,1,0:T(8,128)S(1)}, u32[]{:S(2)}, u32[]{:S(2)}) collective-permute-start(f32[12,8,768]{2,1,0:T(8,128)S(1)} %get-tuple-element.36), channel_id=1, source_target_pairs={{0,129},{1,128},{2,131},{3,130},{4,133},{5,132},{6,135},{7,134},{8... | collective-permute-start | bytes 884744 | tf_op jit(solution)/shard_map/ppermute | solution.py:229
  43.1 8.8 %collective-permute-start.8 = (f32[12,8,768]{2,1,0:T(8,128)S(1)}, f32[12,8,768]{2,1,0:T(8,128)S(1)}, u32[]{:S(2)}, u32[]{:S(2)}) collective-permute-start(f32[12,8,768]{2,1,0:T(8,128)S(1)} %get-tuple-element.34), channel_id=1, source_target_pairs={{0,1},{1,0},{2,3},{3,2},{4,5},{5,4},{6,7},{7,6},{8,9},{9,8},{10,11... | collective-permute-start | bytes 884744 | tf_op jit(solution)/shard_map/ppermute | solution.py:229
where the time goes:
time: 53 us; the launch traced here: 52.8 us
  starting transfers between devices  19.6 us (37%)
  waiting for transfers between devices  19.6 us (37%)
  Pallas kernels  11.8 us (22%)
  local copies, waits for them, and re-layouts  1.71 us (3%)
    ppermute x10, waiting for transfers between devices, send(): return lax.ppermute(x, ('mom', 'energy'), pairs)  19.6 us
    ppermute x10, starting transfers between devices, send(): return lax.ppermute(x, ('mom', 'energy'), pairs)  19.6 us
    pallas_call x3, Pallas kernels, mix_call(): pl.pallas_call(functools.partial(mix_kernel, count, first, moms, keep), o...  9.5 us
    unnamed x10, local copies, waits for them, and re-layouts  1.71 us
    pallas_call x1, Pallas kernels, layer(): pl.pallas_call(prepare_kernel, out_shape=(jax.ShapeDtypeStruct((2 * GROUP...  1.23 us
  transfers between devices with their start and end apart: 10, of which 5 were waited for; matrix products, arithmetic and copies ran while one was open for 0% of the time, Pallas kernels for 20%

commit v1 on v0

--- a/solution.py
+++ b/solution.py
@@ -16,7 +16,7 @@
 NK = 4
 WIDTH = ORB * NA
 PAIRS = WIDTH // 128
-UNROLL_RIGHT = 2
+UNROLL_RIGHT = 6
 GROUP = 4 * HW
 
 PARAMS = pltpu.CompilerParams(vmem_limit_bytes=24 * 1024 * 1024)
@@ -103,8 +103,7 @@
         for i in range(ORB):
             term = left_ref[i, d, pl.ds(start + p, HW, stride=0), :] * picked[i]
             total = term if total is None else total + term
-        half_ref[d, k, p, 0, :, lanes] = total
-        half_ref[d, k, p, 1, :, lanes] = pltpu.roll(total, NA, 1)
+        half_ref[d, k, p, :, lanes] = total
 
 
 def right_products(right_ref, half_ref, outs):
@@ -113,9 +112,8 @@
         def right_side(p, carry):
             sums = [None] * PAIRS
             for d in range(DIRS):
-                plain, swapped = (
-                    [half_ref[d, k, p, n, :, pl.ds(jj * 128, 128)] for jj in range(PAIRS)] for n in range(2)
-                )
+                plain = [half_ref[d, k, p, :, pl.ds(jj * 128, 128)] for jj in range(PAIRS)]
+                swapped = [pltpu.roll(v, NA, 1) for v in plain]
                 for q in range(PAIRS):
                     for jj in range(PAIRS):
                         straight = right_ref[d, jj, 0, pl.ds(q, HW, stride=0), :]
@@ -129,11 +127,10 @@
         lax.fori_loop(0, out_ref.shape[0], right_side, 0, unroll=UNROLL_RIGHT)
 
 
-def mix_kernel(count, first, moms, keep, *refs):
+def mix_kernel(count, first, moms, *refs):
     sources = refs[:count]
     lhs_ref, left_ref, right_ref, pick_ref, *outs = refs[count:-2]
     mixed_ref, half_ref = refs[-2:]
-    kept_ref = outs.pop() if keep else None
     depth = count * HW
     rows = len(moms) * GROUP
 
@@ -173,9 +170,6 @@
                     )
                     for i in range(ORB)
                 ]
-                if keep:
-                    for i in range(ORB):
-                        kept_ref[jj, d, k, i] = picked[i]
                 left_products(picked, left_ref, half_ref, d, k, 0, lanes)
 
     mix(0, 0)
@@ -248,19 +242,17 @@
 BLOCK = jax.ShapeDtypeStruct((ORB, HW, WIDTH), jnp.float32)
 
 
-def mix_call(sources, tables, first, moms, orbitals, keep=False):
+def mix_call(sources, tables, first, moms, orbitals):
     count = len(sources)
     outs = [jax.ShapeDtypeStruct((orbitals, HW, WIDTH), jnp.float32)] * len(moms)
-    if keep:
-        outs.append(jax.ShapeDtypeStruct((PAIRS, DIRS, len(moms), ORB, HW, 128), jnp.float32))
     return pl.pallas_call(
-        functools.partial(mix_kernel, count, first, moms, keep),
+        functools.partial(mix_kernel, count, first, moms),
         out_shape=tuple(outs),
         in_specs=[VMEM] * (count + 4),
         out_specs=(VMEM,) * len(outs),
         scratch_shapes=[
             pltpu.VMEM((2, ORB, len(moms), DIRS, HW, 128), jnp.float32),
-            pltpu.VMEM((DIRS, len(moms), orbitals, 2, HW, WIDTH), jnp.float32),
+            pltpu.VMEM((DIRS, len(moms), orbitals, HW, WIDTH), jnp.float32),
         ],
         compiler_params=PARAMS,
         name="mix",
@@ -276,7 +268,7 @@
         scratch_shapes=STAGED,
         compiler_params=PARAMS,
         name="split",
-    )(green.reshape(HW * 2 * ORB, WIDTH))
+    )(pltpu.with_memory_space_constraint(green.reshape(HW * 2 * ORB, WIDTH), pltpu.MemorySpace.HBM))
     here_far = send(other, stay, 2)
     beyond_own = send(mine, beyond, 0)
     here_near = send(mine, stay, 1)

time: 53 us -> 52.3 us (0.987)
  local copies, waits for them, and re-layouts: 1.71 us -> 0.65 us
  waiting for transfers between devices: 19.6 us -> 20.3 us
    pallas_call x3, Pallas kernels: 9.5 us -> 8.11 us  [mix_call(): pl.pallas_call(functools.partial(mix_kernel, count, first, moms), out_sha...]
    unnamed x10 -> x8, local copies, waits for them, and re-layouts: 1.71 us -> 0.65 us
    pallas_call x1, Pallas kernels: 0.24 us -> 1.24 us  [layer(): pl.pallas_call(split_kernel, out_shape=(BLOCK, BLOCK), in_specs=[HBM], ou...]
    ppermute x10, waiting for transfers between devices: 19.6 us -> 20.3 us  [send(): return lax.ppermute(x, ('mom', 'energy'), pairs)]
  transfers between devices with their start and end apart: 10 -> 10, of which waited for: 5 -> 5; matrix products, arithmetic and copies ran while one was open for 0% -> 0% of each run, Pallas kernels for 20% -> 18%
where the time goes in v1:
time: 52.3 us; the launch traced here: 52.1 us
  waiting for transfers between devices  20.3 us (39%)
  starting transfers between devices  19.6 us (37%)
  Pallas kernels  11.5 us (22%)
  local copies, waits for them, and re-layouts  0.65 us (1%)
    ppermute x10, waiting for transfers between devices, send(): return lax.ppermute(x, ('mom', 'energy'), pairs)  20.3 us
    ppermute x10, starting transfers between devices, send(): return lax.ppermute(x, ('mom', 'energy'), pairs)  19.6 us
    pallas_call x3, Pallas kernels, mix_call(): pl.pallas_call(functools.partial(mix_kernel, count, first, moms), out_sha...  8.11 us
    pallas_call x1, Pallas kernels, layer(): pl.pallas_call(split_kernel, out_shape=(BLOCK, BLOCK), in_specs=[HBM], ou...  1.24 us
    pallas_call x1, Pallas kernels, layer(): pl.pallas_call(prepare_kernel, out_shape=(jax.ShapeDtypeStruct((2 * GROUP...  1.23 us
  transfers between devices with their start and end apart: 10, of which 5 were waited for; matrix products, arithmetic and copies ran while one was open for 0% of the time, Pallas kernels for 18%

profile of v1, /device:TPU:24, one launch (start us, length us, event | category | flops | bytes accessed | tf_op | source)
XLA Modules:
  0.0 52.1 jit_solution(18033082130006554323)
XLA Ops:
  0.0 0.0 copy-start
  0.0 0.0 copy-start.1
  0.0 1.2 %split.1 = (f32[12,8,768]{2,1,0:T(8,128)S(1)}, f32[12,8,768]{2,1,0:T(8,128)S(1)}) custom-call(f32[192,768]{1,0:T(8,128)} %bitcast.6), custom_call_target="tpu_custom_call" | custom-call | tf_op jit(solution)/shard_map/split/pallas_call | solution.py:263
  1.3 0.0 copy-start.2
  1.3 3.1 %collective-permute-start.1 = (f32[12,8,768]{2,1,0:T(8,128)S(1)}, f32[12,8,768]{2,1,0:T(8,128)S(1)}, u32[]{:S(2)}, u32[]{:S(2)}) collective-permute-start(f32[12,8,768]{2,1,0:T(8,128)S(1)} %get-tuple-element.22), channel_id=1, source_target_pairs={{0,128},{1,129},{2,130},{3,131},{4,132},{5,133},{6,134},{7,135},{8... | collective-permute-start | bytes 884744 | tf_op jit(solution)/shard_map/ppermute | solution.py:223
  4.4 0.0 copy-start.3
  4.4 0.0 collective-permute-start
  4.4 0.0 copy-done
  4.4 0.0 copy-done.1
  4.4 0.0 copy-done.2
  4.4 0.6 %copy-done.3 = s32[8]{0:T(128)S(1)} copy-done((s32[8]{0:T(128)S(1)}, s32[8]{0:T(128)}, u32[]{:S(2)}) %copy-start.3) | copy-done | bytes 56
  5.0 1.2 %prepare.1 = (bf16[64,384]{1,0:T(8,128)(2,1)S(1)}, f32[12,3,16,128]{3,2,1,0:T(8,128)S(1)}, f32[3,6,2,8,128]{4,3,2,1,0:T(8,128)S(1)}, s32[8,128]{1,0:T(8,128)S(1)}) custom-call(f32[2,3,4,8]{3,2,1,0:T(4,128)S(1)} %bitcast.5, s32[8]{0:T(128)S(1)} %copy-done.3, s32[3,64]{1,0:T(4,128)S(1)} %copy-done.2, f32[3,12,768]{2,1,0:T(8,128)S(1)} %copy-done), custom_call_target="tpu_custom_call" | custom-call | tf_op jit(solution)/shard_map/prepare/pallas_call | solution.py:275
  6.3 5.3 %collective-permute-done.1.refs_2_ = f32[12,8,768]{2,1,0:T(8,128)S(1)} collective-permute-done((f32[12,8,768]{2,1,0:T(8,128)S(1)}, f32[12,8,768]{2,1,0:T(8,128)S(1)}, u32[]{:S(2)}, u32[]{:S(2)}) %collective-permute-start.1) | collective-permute-done | bytes 294944 | tf_op jit(solution)/shard_map/ppermute | solution.py:223
  11.6 0.0 collective-permute-start.2
  11.6 7.9 %collective-permute-start.3 = (f32[12,8,768]{2,1,0:T(8,128)S(1)}, f32[12,8,768]{2,1,0:T(8,128)S(1)}, u32[]{:S(2)}, u32[]{:S(2)}) collective-permute-start(f32[12,8,768]{2,1,0:T(8,128)S(1)} %get-tuple-element.35.refs_0_), channel_id=1, source_target_pairs={{1,3},{2,0},{3,5},{4,2},{5,7},{6,4},{7,9},{8,6},{9,11},{10,8},{11,... | collective-permute-start | bytes 884744 | tf_op jit(solution)/shard_map/ppermute | solution.py:223
  19.6 2.9 %collective-permute-start.4 = (f32[12,8,768]{2,1,0:T(8,128)S(1)}, f32[12,8,768]{2,1,0:T(8,128)S(1)}, u32[]{:S(2)}, u32[]{:S(2)}) collective-permute-start(f32[12,8,768]{2,1,0:T(8,128)S(1)} %collective-permute-done.1.refs_2_), channel_id=1, source_target_pairs={{1,3},{2,0},{3,5},{4,2},{5,7},{6,4},{7,9},{8,6},{9,11},{10,8},{11,... | collective-permute-start | bytes 884744 | tf_op jit(solution)/shard_map/ppermute | solution.py:223
  22.5 0.0 collective-permute-done.refs_1_
  22.5 0.0 collective-permute-done.2.refs_3_
  22.5 2.0 %mix.3 = f32[12,8,768]{2,1,0:T(8,128)S(1)} custom-call(f32[12,8,768]{2,1,0:T(8,128)S(1)} %get-tuple-element.35.refs_0_, f32[12,8,768]{2,1,0:T(8,128)S(1)} %collective-permute-done.refs_1_, f32[12,8,768]{2,1,0:T(8,128)S(1)} %collective-permute-done.1.refs_2_, f32[12,8,768]{2,1,0:T(8,128)S(1)} %collective-permute-done.2.refs_3_, ...), custom_call_target="tpu_custom_call" | custom-call | tf_op jit(solution)/shard_map/mix/pallas_call | solution.py:248
  24.5 2.4 %collective-permute-done.3.refs_4_ = f32[12,8,768]{2,1,0:T(8,128)S(1)} collective-permute-done((f32[12,8,768]{2,1,0:T(8,128)S(1)}, f32[12,8,768]{2,1,0:T(8,128)S(1)}, u32[]{:S(2)}, u32[]{:S(2)}) %collective-permute-start.3) | collective-permute-done | bytes 294944 | tf_op jit(solution)/shard_map/ppermute | solution.py:223
  26.9 5.9 %collective-permute-done.4.refs_6_ = f32[12,8,768]{2,1,0:T(8,128)S(1)} collective-permute-done((f32[12,8,768]{2,1,0:T(8,128)S(1)}, f32[12,8,768]{2,1,0:T(8,128)S(1)}, u32[]{:S(2)}, u32[]{:S(2)}) %collective-permute-start.4) | collective-permute-done | bytes 294944 | tf_op jit(solution)/shard_map/ppermute | solution.py:223
  32.8 0.0 collective-permute-start.5
  32.8 0.5 collective-permute-start.6
  33.3 3.0 %collective-permute-start.7 = (f32[12,8,768]{2,1,0:T(8,128)S(1)}, f32[12,8,768]{2,1,0:T(8,128)S(1)}, u32[]{:S(2)}, u32[]{:S(2)}) collective-permute-start(f32[12,8,768]{2,1,0:T(8,128)S(1)} %mix.3), channel_id=1, source_target_pairs={{0,128},{1,129},{2,130},{3,131},{4,132},{5,133},{6,134},{7,135},{8... | collective-permute-start | bytes 884744 | tf_op jit(solution)/shard_map/ppermute | solution.py:223
  36.3 0.0 collective-permute-done.5.refs_5_
  36.3 0.0 collective-permute-done.6.refs_7_
  36.3 4.1 %mix.4 = (f32[12,8,768]{2,1,0:T(8,128)S(1)}, f32[12,8,768]{2,1,0:T(8,128)S(1)}) custom-call(f32[12,8,768]{2,1,0:T(8,128)S(1)} %get-tuple-element.35.refs_0_, f32[12,8,768]{2,1,0:T(8,128)S(1)} %collective-permute-done.refs_1_, f32[12,8,768]{2,1,0:T(8,128)S(1)} %collective-permute-done.1.refs_2_, f32[12,8,768]{2,1,0:T(8,128)S(1)} %collective-permute-done.2.refs_3_, ...), custom_call_target="tpu_custom_call" | custom-call | tf_op jit(solution)/shard_map/mix/pallas_call | solution.py:248
  40.4 2.1 %collective-permute-start.9 = (f32[12,8,768]{2,1,0:T(8,128)S(1)}, f32[12,8,768]{2,1,0:T(8,128)S(1)}, u32[]{:S(2)}, u32[]{:S(2)}) collective-permute-start(f32[12,8,768]{2,1,0:T(8,128)S(1)} %get-tuple-element.36), channel_id=1, source_target_pairs={{0,129},{1,128},{2,131},{3,130},{4,133},{5,132},{6,135},{7,134},{8... | collective-permute-start | bytes 884744 | tf_op jit(solution)/shard_map/ppermute | solution.py:223
  42.5 0.0 collective-permute-start.8
  42.5 2.0 %mix.5.own_ref = f32[12,8,768]{2,1,0:T(8,128)S(1)} custom-call(f32[12,8,768]{2,1,0:T(8,128)S(1)} %get-tuple-element.35.refs_0_, f32[12,8,768]{2,1,0:T(8,128)S(1)} %collective-permute-done.refs_1_, f32[12,8,768]{2,1,0:T(8,128)S(1)} %collective-permute-done.1.refs_2_, f32[12,8,768]{2,1,0:T(8,128)S(1)} %collective-permute-done.2.refs_3_, ...), custom_call_target="tpu_custom_call" | custom-call | tf_op jit(solution)/shard_map/mix/pallas_call | solution.py:248
  44.5 0.0 collective-permute-done.7.far_ref
  44.5 5.8 %collective-permute-done.9.far_edge_ref = f32[12,8,768]{2,1,0:T(8,128)S(1)} collective-permute-done((f32[12,8,768]{2,1,0:T(8,128)S(1)}, f32[12,8,768]{2,1,0:T(8,128)S(1)}, u32[]{:S(2)}, u32[]{:S(2)}) %collective-permute-start.9) | collective-permute-done | bytes 294944 | tf_op jit(solution)/shard_map/ppermute | solution.py:223
  50.3 0.9 %collective-permute-done.8.near_edge_ref = f32[12,8,768]{2,1,0:T(8,128)S(1)} collective-permute-done((f32[12,8,768]{2,1,0:T(8,128)S(1)}, f32[12,8,768]{2,1,0:T(8,128)S(1)}, u32[]{:S(2)}, u32[]{:S(2)}) %collective-permute-start.8) | collective-permute-done | bytes 294944 | tf_op jit(solution)/shard_map/ppermute | solution.py:223
  51.2 0.9 %join.1 = f32[192,768]{1,0:T(8,128)} custom-call(f32[12,8,768]{2,1,0:T(8,128)S(1)} %mix.5.own_ref, f32[12,8,768]{2,1,0:T(8,128)S(1)} %collective-permute-done.7.far_ref, f32[12,8,768]{2,1,0:T(8,128)S(1)} %collective-permute-done.8.near_edge_ref, f32[12,8,768]{2,1,0:T(8,128)S(1)} %collective-permute-done.9.far_edge_ref), custom_call_target="tpu_custom_call" | custom-call | tf_op jit(solution)/shard_map/join/pallas_call | solution.py:301
Async XLA Ops:
  0.0 4.4 %copy-start = (f32[3,12,768]{2,1,0:T(8,128)S(1)}, f32[3,12,768]{2,1,0:T(8,128)}, u32[]{:S(2)}) copy-start(f32[3,12,768]{2,1,0:T(8,128)} %gradients_ref.1) | copy-start | bytes 331780
  0.0 4.4 %copy-start.1 = (f32[2,3,8,4]{2,3,1,0:T(4,128)S(1)}, f32[2,3,8,4]{2,3,1,0:T(4,128)}, u32[]{:S(2)}) copy-start(f32[2,3,8,4]{2,3,1,0:T(4,128)} %param.8) | copy-start | bytes 2308
  1.3 3.1 %copy-start.2 = (s32[3,64]{1,0:T(4,128)S(1)}, s32[3,64]{1,0:T(4,128)}, u32[]{:S(2)}) copy-start(s32[3,64]{1,0:T(4,128)} %neighbours_ref.1) | copy-start | bytes 2308
  1.3 10.3 %collective-permute-start.1 = (f32[12,8,768]{2,1,0:T(8,128)S(1)}, f32[12,8,768]{2,1,0:T(8,128)S(1)}, u32[]{:S(2)}, u32[]{:S(2)}) collective-permute-start(f32[12,8,768]{2,1,0:T(8,128)S(1)} %get-tuple-element.22), channel_id=1, source_target_pairs={{0,128},{1,129},{2,130},{3,131},{4,132},{5,133},{6,134},{7,135},{8... | collective-permute-start | bytes 884744 | tf_op jit(solution)/shard_map/ppermute | solution.py:223
  4.4 0.7 %copy-start.3 = (s32[8]{0:T(128)S(1)}, s32[8]{0:T(128)}, u32[]{:S(2)}) copy-start(s32[8]{0:T(128)} %offsets_ref.1) | copy-start | bytes 100
  4.4 18.1 %collective-permute-start = (f32[12,8,768]{2,1,0:T(8,128)S(1)}, f32[12,8,768]{2,1,0:T(8,128)S(1)}, u32[]{:S(2)}, u32[]{:S(2)}) collective-permute-start(f32[12,8,768]{2,1,0:T(8,128)S(1)} %get-tuple-element.35.refs_0_), channel_id=1, source_target_pairs={{0,64},{1,65},{2,66},{3,67},{4,68},{5,69},{6,70},{7,71},{8,72},{9,... | collective-permute-start | bytes 884744 | tf_op jit(solution)/shard_map/ppermute | solution.py:223
  11.6 10.9 %collective-permute-start.2 = (f32[12,8,768]{2,1,0:T(8,128)S(1)}, f32[12,8,768]{2,1,0:T(8,128)S(1)}, u32[]{:S(2)}, u32[]{:S(2)}) collective-permute-start(f32[12,8,768]{2,1,0:T(8,128)S(1)} %collective-permute-done.1.refs_2_), channel_id=1, source_target_pairs={{0,64},{1,65},{2,66},{3,67},{4,68},{5,69},{6,70},{7,71},{8,72},{9,... | collective-permute-start | bytes 884744 | tf_op jit(solution)/shard_map/ppermute | solution.py:223
  11.6 15.3 %collective-permute-start.3 = (f32[12,8,768]{2,1,0:T(8,128)S(1)}, f32[12,8,768]{2,1,0:T(8,128)S(1)}, u32[]{:S(2)}, u32[]{:S(2)}) collective-permute-start(f32[12,8,768]{2,1,0:T(8,128)S(1)} %get-tuple-element.35.refs_0_), channel_id=1, source_target_pairs={{1,3},{2,0},{3,5},{4,2},{5,7},{6,4},{7,9},{8,6},{9,11},{10,8},{11,... | collective-permute-start | bytes 884744 | tf_op jit(solution)/shard_map/ppermute | solution.py:223
  19.6 13.2 %collective-permute-start.4 = (f32[12,8,768]{2,1,0:T(8,128)S(1)}, f32[12,8,768]{2,1,0:T(8,128)S(1)}, u32[]{:S(2)}, u32[]{:S(2)}) collective-permute-start(f32[12,8,768]{2,1,0:T(8,128)S(1)} %collective-permute-done.1.refs_2_), channel_id=1, source_target_pairs={{1,3},{2,0},{3,5},{4,2},{5,7},{6,4},{7,9},{8,6},{9,11},{10,8},{11,... | collective-permute-start | bytes 884744 | tf_op jit(solution)/shard_map/ppermute | solution.py:223
  32.8 3.5 %collective-permute-start.5 = (f32[12,8,768]{2,1,0:T(8,128)S(1)}, f32[12,8,768]{2,1,0:T(8,128)S(1)}, u32[]{:S(2)}, u32[]{:S(2)}) collective-permute-start(f32[12,8,768]{2,1,0:T(8,128)S(1)} %collective-permute-done.3.refs_4_), channel_id=1, source_target_pairs={{0,64},{1,65},{2,66},{3,67},{4,68},{5,69},{6,70},{7,71},{8,72},{9,... | collective-permute-start | bytes 884744 | tf_op jit(solution)/shard_map/ppermute | solution.py:223
  32.8 3.5 %collective-permute-start.6 = (f32[12,8,768]{2,1,0:T(8,128)S(1)}, f32[12,8,768]{2,1,0:T(8,128)S(1)}, u32[]{:S(2)}, u32[]{:S(2)}) collective-permute-start(f32[12,8,768]{2,1,0:T(8,128)S(1)} %collective-permute-done.4.refs_6_), channel_id=1, source_target_pairs={{0,64},{1,65},{2,66},{3,67},{4,68},{5,69},{6,70},{7,71},{8,72},{9,... | collective-permute-start | bytes 884744 | tf_op jit(solution)/shard_map/ppermute | solution.py:223
  33.3 11.2 %collective-permute-start.7 = (f32[12,8,768]{2,1,0:T(8,128)S(1)}, f32[12,8,768]{2,1,0:T(8,128)S(1)}, u32[]{:S(2)}, u32[]{:S(2)}) collective-permute-start(f32[12,8,768]{2,1,0:T(8,128)S(1)} %mix.3), channel_id=1, source_target_pairs={{0,128},{1,129},{2,130},{3,131},{4,132},{5,133},{6,134},{7,135},{8... | collective-permute-start | bytes 884744 | tf_op jit(solution)/shard_map/ppermute | solution.py:223
  40.4 9.9 %collective-permute-start.9 = (f32[12,8,768]{2,1,0:T(8,128)S(1)}, f32[12,8,768]{2,1,0:T(8,128)S(1)}, u32[]{:S(2)}, u32[]{:S(2)}) collective-permute-start(f32[12,8,768]{2,1,0:T(8,128)S(1)} %get-tuple-element.36), channel_id=1, source_target_pairs={{0,129},{1,128},{2,131},{3,130},{4,133},{5,132},{6,135},{7,134},{8... | collective-permute-start | bytes 884744 | tf_op jit(solution)/shard_map/ppermute | solution.py:223
  42.5 8.8 %collective-permute-start.8 = (f32[12,8,768]{2,1,0:T(8,128)S(1)}, f32[12,8,768]{2,1,0:T(8,128)S(1)}, u32[]{:S(2)}, u32[]{:S(2)}) collective-permute-start(f32[12,8,768]{2,1,0:T(8,128)S(1)} %get-tuple-element.34), channel_id=1, source_target_pairs={{0,1},{1,0},{2,3},{3,2},{4,5},{5,4},{6,7},{7,6},{8,9},{9,8},{10,11... | collective-permute-start | bytes 884744 | tf_op jit(solution)/shard_map/ppermute | solution.py:223

commit v2 on v1

--- a/solution.py
+++ b/solution.py
@@ -16,7 +16,7 @@
 NK = 4
 WIDTH = ORB * NA
 PAIRS = WIDTH // 128
-UNROLL_RIGHT = 6
+UNROLL_RIGHT = 12
 GROUP = 4 * HW
 
 PARAMS = pltpu.CompilerParams(vmem_limit_bytes=24 * 1024 * 1024)
@@ -295,7 +295,8 @@
     far = send(far, stay, 2)
     there = [beyond_own, send(beyond_own, stay, 1), beyond_far, send(beyond_far, stay, 1)]
     near_edge, far_edge = mix_call(here + there, tables, 0, (0, 1), ORB)
-    edges = [send(near_edge, pair, 0), send(far_edge, pair, 2)]
+    near_sent = send(near_edge, pair, 0)
+    edges = [near_sent, send(far_edge, pair, 2)]
     here[0], near_edge = lax.optimization_barrier((mine, near_edge))
     (own,) = mix_call(here, tables, 256, (0,), ORB)
     out = pl.pallas_call(

time: 52.3 us -> 52.1 us (level)
  transfers between devices with their start and end apart: 10 -> 10, of which waited for: 5 -> 5; matrix products, arithmetic and copies ran while one was open for 0% -> 0% of each run, Pallas kernels for 18% -> 17%
where the time goes in v2:
time: 52.1 us; the launch traced here: 51.9 us
  waiting for transfers between devices  20.4 us (39%)
  starting transfers between devices  19.6 us (38%)
  Pallas kernels  11.2 us (21%)
  local copies, waits for them, and re-layouts  0.65 us (1%)
    ppermute x10, waiting for transfers between devices, send(): return lax.ppermute(x, ('mom', 'energy'), pairs)  20.4 us
    ppermute x10, starting transfers between devices, send(): return lax.ppermute(x, ('mom', 'energy'), pairs)  19.6 us
    pallas_call x3, Pallas kernels, mix_call(): pl.pallas_call(functools.partial(mix_kernel, count, first, moms), out_sha...  7.82 us
    pallas_call x1, Pallas kernels, layer(): pl.pallas_call(split_kernel, out_shape=(BLOCK, BLOCK), in_specs=[HBM], ou...  1.24 us
    pallas_call x1, Pallas kernels, layer(): pl.pallas_call(prepare_kernel, out_shape=(jax.ShapeDtypeStruct((2 * GROUP...  1.23 us
  transfers between devices with their start and end apart: 10, of which 5 were waited for; matrix products, arithmetic and copies ran while one was open for 0% of the time, Pallas kernels for 17%

profile of v2, /device:TPU:24, one launch (start us, length us, event | category | flops | bytes accessed | tf_op | source)
XLA Modules:
  0.0 51.9 jit_solution(8373608419812818668)
XLA Ops:
  0.0 0.0 copy-start
  0.0 0.0 copy-start.1
  0.0 1.2 %split.1 = (f32[12,8,768]{2,1,0:T(8,128)S(1)}, f32[12,8,768]{2,1,0:T(8,128)S(1)}) custom-call(f32[192,768]{1,0:T(8,128)} %bitcast.6), custom_call_target="tpu_custom_call" | custom-call | tf_op jit(solution)/shard_map/split/pallas_call | solution.py:263
  1.3 0.0 copy-start.2
  1.3 3.1 %collective-permute-start.1 = (f32[12,8,768]{2,1,0:T(8,128)S(1)}, f32[12,8,768]{2,1,0:T(8,128)S(1)}, u32[]{:S(2)}, u32[]{:S(2)}) collective-permute-start(f32[12,8,768]{2,1,0:T(8,128)S(1)} %get-tuple-element.22), channel_id=1, source_target_pairs={{0,128},{1,129},{2,130},{3,131},{4,132},{5,133},{6,134},{7,135},{8... | collective-permute-start | bytes 884744 | tf_op jit(solution)/shard_map/ppermute | solution.py:223
  4.4 0.0 copy-start.3
  4.4 0.0 collective-permute-start
  4.4 0.0 copy-done
  4.4 0.0 copy-done.1
  4.4 0.0 copy-done.2
  4.4 0.6 %copy-done.3 = s32[8]{0:T(128)S(1)} copy-done((s32[8]{0:T(128)S(1)}, s32[8]{0:T(128)}, u32[]{:S(2)}) %copy-start.3) | copy-done | bytes 56
  5.0 1.2 %prepare.1 = (bf16[64,384]{1,0:T(8,128)(2,1)S(1)}, f32[12,3,16,128]{3,2,1,0:T(8,128)S(1)}, f32[3,6,2,8,128]{4,3,2,1,0:T(8,128)S(1)}, s32[8,128]{1,0:T(8,128)S(1)}) custom-call(f32[2,3,4,8]{3,2,1,0:T(4,128)S(1)} %bitcast.5, s32[8]{0:T(128)S(1)} %copy-done.3, s32[3,64]{1,0:T(4,128)S(1)} %copy-done.2, f32[3,12,768]{2,1,0:T(8,128)S(1)} %copy-done), custom_call_target="tpu_custom_call" | custom-call | tf_op jit(solution)/shard_map/prepare/pallas_call | solution.py:275
  6.3 5.3 %collective-permute-done.1.refs_2_ = f32[12,8,768]{2,1,0:T(8,128)S(1)} collective-permute-done((f32[12,8,768]{2,1,0:T(8,128)S(1)}, f32[12,8,768]{2,1,0:T(8,128)S(1)}, u32[]{:S(2)}, u32[]{:S(2)}) %collective-permute-start.1) | collective-permute-done | bytes 294944 | tf_op jit(solution)/shard_map/ppermute | solution.py:223
  11.6 0.0 collective-permute-start.2
  11.6 7.9 %collective-permute-start.3 = (f32[12,8,768]{2,1,0:T(8,128)S(1)}, f32[12,8,768]{2,1,0:T(8,128)S(1)}, u32[]{:S(2)}, u32[]{:S(2)}) collective-permute-start(f32[12,8,768]{2,1,0:T(8,128)S(1)} %get-tuple-element.35.refs_0_), channel_id=1, source_target_pairs={{1,3},{2,0},{3,5},{4,2},{5,7},{6,4},{7,9},{8,6},{9,11},{10,8},{11,... | collective-permute-start | bytes 884744 | tf_op jit(solution)/shard_map/ppermute | solution.py:223
  19.6 2.9 %collective-permute-start.4 = (f32[12,8,768]{2,1,0:T(8,128)S(1)}, f32[12,8,768]{2,1,0:T(8,128)S(1)}, u32[]{:S(2)}, u32[]{:S(2)}) collective-permute-start(f32[12,8,768]{2,1,0:T(8,128)S(1)} %collective-permute-done.1.refs_2_), channel_id=1, source_target_pairs={{1,3},{2,0},{3,5},{4,2},{5,7},{6,4},{7,9},{8,6},{9,11},{10,8},{11,... | collective-permute-start | bytes 884744 | tf_op jit(solution)/shard_map/ppermute | solution.py:223
  22.5 0.0 collective-permute-done.refs_1_
  22.5 0.0 collective-permute-done.2.refs_3_
  22.5 2.0 %mix.3 = f32[12,8,768]{2,1,0:T(8,128)S(1)} custom-call(f32[12,8,768]{2,1,0:T(8,128)S(1)} %get-tuple-element.35.refs_0_, f32[12,8,768]{2,1,0:T(8,128)S(1)} %collective-permute-done.refs_1_, f32[12,8,768]{2,1,0:T(8,128)S(1)} %collective-permute-done.1.refs_2_, f32[12,8,768]{2,1,0:T(8,128)S(1)} %collective-permute-done.2.refs_3_, ...), custom_call_target="tpu_custom_call" | custom-call | tf_op jit(solution)/shard_map/mix/pallas_call | solution.py:248
  24.5 2.5 %collective-permute-done.3.refs_4_ = f32[12,8,768]{2,1,0:T(8,128)S(1)} collective-permute-done((f32[12,8,768]{2,1,0:T(8,128)S(1)}, f32[12,8,768]{2,1,0:T(8,128)S(1)}, u32[]{:S(2)}, u32[]{:S(2)}) %collective-permute-start.3) | collective-permute-done | bytes 294944 | tf_op jit(solution)/shard_map/ppermute | solution.py:223
  26.9 5.9 %collective-permute-done.4.refs_6_ = f32[12,8,768]{2,1,0:T(8,128)S(1)} collective-permute-done((f32[12,8,768]{2,1,0:T(8,128)S(1)}, f32[12,8,768]{2,1,0:T(8,128)S(1)}, u32[]{:S(2)}, u32[]{:S(2)}) %collective-permute-start.4) | collective-permute-done | bytes 294944 | tf_op jit(solution)/shard_map/ppermute | solution.py:223
  32.8 0.0 collective-permute-start.5
  32.8 0.5 collective-permute-start.6
  33.3 3.0 %collective-permute-start.7 = (f32[12,8,768]{2,1,0:T(8,128)S(1)}, f32[12,8,768]{2,1,0:T(8,128)S(1)}, u32[]{:S(2)}, u32[]{:S(2)}) collective-permute-start(f32[12,8,768]{2,1,0:T(8,128)S(1)} %mix.3), channel_id=1, source_target_pairs={{0,128},{1,129},{2,130},{3,131},{4,132},{5,133},{6,134},{7,135},{8... | collective-permute-start | bytes 884744 | tf_op jit(solution)/shard_map/ppermute | solution.py:223
  36.3 0.0 collective-permute-done.5.refs_5_
  36.3 0.0 collective-permute-done.6.refs_7_
  36.3 3.9 %mix.4 = (f32[12,8,768]{2,1,0:T(8,128)S(1)}, f32[12,8,768]{2,1,0:T(8,128)S(1)}) custom-call(f32[12,8,768]{2,1,0:T(8,128)S(1)} %get-tuple-element.35.refs_0_, f32[12,8,768]{2,1,0:T(8,128)S(1)} %collective-permute-done.refs_1_, f32[12,8,768]{2,1,0:T(8,128)S(1)} %collective-permute-done.1.refs_2_, f32[12,8,768]{2,1,0:T(8,128)S(1)} %collective-permute-done.2.refs_3_, ...), custom_call_target="tpu_custom_call" | custom-call | tf_op jit(solution)/shard_map/mix/pallas_call | solution.py:248
  40.2 2.1 %collective-permute-start.9 = (f32[12,8,768]{2,1,0:T(8,128)S(1)}, f32[12,8,768]{2,1,0:T(8,128)S(1)}, u32[]{:S(2)}, u32[]{:S(2)}) collective-permute-start(f32[12,8,768]{2,1,0:T(8,128)S(1)} %get-tuple-element.36), channel_id=1, source_target_pairs={{0,129},{1,128},{2,131},{3,130},{4,133},{5,132},{6,135},{7,134},{8... | collective-permute-start | bytes 884744 | tf_op jit(solution)/shard_map/ppermute | solution.py:223
  42.3 0.0 collective-permute-start.8
  42.3 2.0 %mix.5.own_ref = f32[12,8,768]{2,1,0:T(8,128)S(1)} custom-call(f32[12,8,768]{2,1,0:T(8,128)S(1)} %get-tuple-element.35.refs_0_, f32[12,8,768]{2,1,0:T(8,128)S(1)} %collective-permute-done.refs_1_, f32[12,8,768]{2,1,0:T(8,128)S(1)} %collective-permute-done.1.refs_2_, f32[12,8,768]{2,1,0:T(8,128)S(1)} %collective-permute-done.2.refs_3_, ...), custom_call_target="tpu_custom_call" | custom-call | tf_op jit(solution)/shard_map/mix/pallas_call | solution.py:248
  44.3 0.0 collective-permute-done.7.far_ref
  44.3 5.9 %collective-permute-done.9.far_edge_ref = f32[12,8,768]{2,1,0:T(8,128)S(1)} collective-permute-done((f32[12,8,768]{2,1,0:T(8,128)S(1)}, f32[12,8,768]{2,1,0:T(8,128)S(1)}, u32[]{:S(2)}, u32[]{:S(2)}) %collective-permute-start.9) | collective-permute-done | bytes 294944 | tf_op jit(solution)/shard_map/ppermute | solution.py:223
  50.1 0.9 %collective-permute-done.8.near_edge_ref = f32[12,8,768]{2,1,0:T(8,128)S(1)} collective-permute-done((f32[12,8,768]{2,1,0:T(8,128)S(1)}, f32[12,8,768]{2,1,0:T(8,128)S(1)}, u32[]{:S(2)}, u32[]{:S(2)}) %collective-permute-start.8) | collective-permute-done | bytes 294944 | tf_op jit(solution)/shard_map/ppermute | solution.py:223
  51.0 0.9 %join.1 = f32[192,768]{1,0:T(8,128)} custom-call(f32[12,8,768]{2,1,0:T(8,128)S(1)} %mix.5.own_ref, f32[12,8,768]{2,1,0:T(8,128)S(1)} %collective-permute-done.7.far_ref, f32[12,8,768]{2,1,0:T(8,128)S(1)} %collective-permute-done.8.near_edge_ref, f32[12,8,768]{2,1,0:T(8,128)S(1)} %collective-permute-done.9.far_edge_ref), custom_call_target="tpu_custom_call" | custom-call | tf_op jit(solution)/shard_map/join/pallas_call | solution.py:302
Async XLA Ops:
  0.0 4.4 %copy-start = (f32[3,12,768]{2,1,0:T(8,128)S(1)}, f32[3,12,768]{2,1,0:T(8,128)}, u32[]{:S(2)}) copy-start(f32[3,12,768]{2,1,0:T(8,128)} %gradients_ref.1) | copy-start | bytes 331780
  0.0 4.4 %copy-start.1 = (f32[2,3,8,4]{2,3,1,0:T(4,128)S(1)}, f32[2,3,8,4]{2,3,1,0:T(4,128)}, u32[]{:S(2)}) copy-start(f32[2,3,8,4]{2,3,1,0:T(4,128)} %param.8) | copy-start | bytes 2308
  1.3 3.1 %copy-start.2 = (s32[3,64]{1,0:T(4,128)S(1)}, s32[3,64]{1,0:T(4,128)}, u32[]{:S(2)}) copy-start(s32[3,64]{1,0:T(4,128)} %neighbours_ref.1) | copy-start | bytes 2308
  1.3 10.3 %collective-permute-start.1 = (f32[12,8,768]{2,1,0:T(8,128)S(1)}, f32[12,8,768]{2,1,0:T(8,128)S(1)}, u32[]{:S(2)}, u32[]{:S(2)}) collective-permute-start(f32[12,8,768]{2,1,0:T(8,128)S(1)} %get-tuple-element.22), channel_id=1, source_target_pairs={{0,128},{1,129},{2,130},{3,131},{4,132},{5,133},{6,134},{7,135},{8... | collective-permute-start | bytes 884744 | tf_op jit(solution)/shard_map/ppermute | solution.py:223
  4.4 0.7 %copy-start.3 = (s32[8]{0:T(128)S(1)}, s32[8]{0:T(128)}, u32[]{:S(2)}) copy-start(s32[8]{0:T(128)} %offsets_ref.1) | copy-start | bytes 100
  4.4 18.1 %collective-permute-start = (f32[12,8,768]{2,1,0:T(8,128)S(1)}, f32[12,8,768]{2,1,0:T(8,128)S(1)}, u32[]{:S(2)}, u32[]{:S(2)}) collective-permute-start(f32[12,8,768]{2,1,0:T(8,128)S(1)} %get-tuple-element.35.refs_0_), channel_id=1, source_target_pairs={{0,64},{1,65},{2,66},{3,67},{4,68},{5,69},{6,70},{7,71},{8,72},{9,... | collective-permute-start | bytes 884744 | tf_op jit(solution)/shard_map/ppermute | solution.py:223
  11.6 10.9 %collective-permute-start.2 = (f32[12,8,768]{2,1,0:T(8,128)S(1)}, f32[12,8,768]{2,1,0:T(8,128)S(1)}, u32[]{:S(2)}, u32[]{:S(2)}) collective-permute-start(f32[12,8,768]{2,1,0:T(8,128)S(1)} %collective-permute-done.1.refs_2_), channel_id=1, source_target_pairs={{0,64},{1,65},{2,66},{3,67},{4,68},{5,69},{6,70},{7,71},{8,72},{9,... | collective-permute-start | bytes 884744 | tf_op jit(solution)/shard_map/ppermute | solution.py:223
  11.6 15.3 %collective-permute-start.3 = (f32[12,8,768]{2,1,0:T(8,128)S(1)}, f32[12,8,768]{2,1,0:T(8,128)S(1)}, u32[]{:S(2)}, u32[]{:S(2)}) collective-permute-start(f32[12,8,768]{2,1,0:T(8,128)S(1)} %get-tuple-element.35.refs_0_), channel_id=1, source_target_pairs={{1,3},{2,0},{3,5},{4,2},{5,7},{6,4},{7,9},{8,6},{9,11},{10,8},{11,... | collective-permute-start | bytes 884744 | tf_op jit(solution)/shard_map/ppermute | solution.py:223
  19.6 13.2 %collective-permute-start.4 = (f32[12,8,768]{2,1,0:T(8,128)S(1)}, f32[12,8,768]{2,1,0:T(8,128)S(1)}, u32[]{:S(2)}, u32[]{:S(2)}) collective-permute-start(f32[12,8,768]{2,1,0:T(8,128)S(1)} %collective-permute-done.1.refs_2_), channel_id=1, source_target_pairs={{1,3},{2,0},{3,5},{4,2},{5,7},{6,4},{7,9},{8,6},{9,11},{10,8},{11,... | collective-permute-start | bytes 884744 | tf_op jit(solution)/shard_map/ppermute | solution.py:223
  32.8 3.5 %collective-permute-start.5 = (f32[12,8,768]{2,1,0:T(8,128)S(1)}, f32[12,8,768]{2,1,0:T(8,128)S(1)}, u32[]{:S(2)}, u32[]{:S(2)}) collective-permute-start(f32[12,8,768]{2,1,0:T(8,128)S(1)} %collective-permute-done.3.refs_4_), channel_id=1, source_target_pairs={{0,64},{1,65},{2,66},{3,67},{4,68},{5,69},{6,70},{7,71},{8,72},{9,... | collective-permute-start | bytes 884744 | tf_op jit(solution)/shard_map/ppermute | solution.py:223
  32.8 3.5 %collective-permute-start.6 = (f32[12,8,768]{2,1,0:T(8,128)S(1)}, f32[12,8,768]{2,1,0:T(8,128)S(1)}, u32[]{:S(2)}, u32[]{:S(2)}) collective-permute-start(f32[12,8,768]{2,1,0:T(8,128)S(1)} %collective-permute-done.4.refs_6_), channel_id=1, source_target_pairs={{0,64},{1,65},{2,66},{3,67},{4,68},{5,69},{6,70},{7,71},{8,72},{9,... | collective-permute-start | bytes 884744 | tf_op jit(solution)/shard_map/ppermute | solution.py:223
  33.3 11.0 %collective-permute-start.7 = (f32[12,8,768]{2,1,0:T(8,128)S(1)}, f32[12,8,768]{2,1,0:T(8,128)S(1)}, u32[]{:S(2)}, u32[]{:S(2)}) collective-permute-start(f32[12,8,768]{2,1,0:T(8,128)S(1)} %mix.3), channel_id=1, source_target_pairs={{0,128},{1,129},{2,130},{3,131},{4,132},{5,133},{6,134},{7,135},{8... | collective-permute-start | bytes 884744 | tf_op jit(solution)/shard_map/ppermute | solution.py:223
  40.2 9.9 %collective-permute-start.9 = (f32[12,8,768]{2,1,0:T(8,128)S(1)}, f32[12,8,768]{2,1,0:T(8,128)S(1)}, u32[]{:S(2)}, u32[]{:S(2)}) collective-permute-start(f32[12,8,768]{2,1,0:T(8,128)S(1)} %get-tuple-element.36), channel_id=1, source_target_pairs={{0,129},{1,128},{2,131},{3,130},{4,133},{5,132},{6,135},{7,134},{8... | collective-permute-start | bytes 884744 | tf_op jit(solution)/shard_map/ppermute | solution.py:223
  42.3 8.8 %collective-permute-start.8 = (f32[12,8,768]{2,1,0:T(8,128)S(1)}, f32[12,8,768]{2,1,0:T(8,128)S(1)}, u32[]{:S(2)}, u32[]{:S(2)}) collective-permute-start(f32[12,8,768]{2,1,0:T(8,128)S(1)} %get-tuple-element.34), channel_id=1, source_target_pairs={{0,1},{1,0},{2,3},{3,2},{4,5},{5,4},{6,7},{7,6},{8,9},{9,8},{10,11... | collective-permute-start | bytes 884744 | tf_op jit(solution)/shard_map/ppermute | solution.py:223
